TPU v7x, 512 devices: a whole 4x8x8 slice. The times are simulated.
512 devices in a mesh: seq: 64 (over x, z, core), head: 8 (over y).
Axes of the slice: x: 4, y: 8, z: 8, core: 2. Of those that a mesh axis runs over, the one named last changes fastest.
Arguments:
- queries: bfloat16 [16384, 4096], P('seq', 'head'), may hold values from -6 to 6
- keys: bfloat16 [16384, 4096], P('seq', 'head'), may hold values from -6 to 6
- values: bfloat16 [16384, 4096], P('seq', 'head'), may hold values from -6 to 6
- gate: bfloat16 [16384, 4096], P('seq', 'head'), may hold values from -6 to 6
- residual: bfloat16 [16384, 4096], P('seq', 'head'), may hold values from -40 to 40
- log_decay: float32 [16384, 32], P('seq', 'head'), may hold values from -1 to 0, as said below
- out_weight: bfloat16 [4096, 4096], P('seq', 'head'), may hold values from -0.09375 to 0.09375
- norm_gain: bfloat16 [4096], P('head'), may hold values from 0.099609375 to 1.8984375
- kv_weight: bfloat16 [4096, 2048], P('seq', 'head'), may hold values from -0.09375 to 0.09375
Outputs:
- cache_keys: bfloat16 [16384, 1024], P('seq', 'head')
- cache_values: bfloat16 [16384, 1024], P('seq', 'head')
Inputs may be any that keep to these rules, and one draw needn't show every extreme that they name: `log_decay`: every entry is negative.
All inputs are finite; a program needn't handle non-finite values.
Results may differ from a plain program's by a relative error of at most 0.015.
Values may be sent and summed in bfloat16 or wider, within the bound.
A program may use at most 64 MiB of HBM per device.

v0:
```python
import jax
import jax.numpy as jnp
from jax import lax
from jax.sharding import PartitionSpec as P

HIGHEST = lax.Precision.HIGHEST


def entering(part, axis, combine, identity):
    place = lax.axis_index(axis)
    gathered = jax.tree.map(lambda a: lax.all_gather(a, axis), part)
    state = jax.tree.map(lambda a, e: jnp.zeros_like(a) + jnp.asarray(e, a.dtype), part, identity)

    def one(step, state):
        return combine(
            state, jax.tree.map(lambda a: lax.dynamic_index_in_dim(a, step, 0, False), gathered)
        )

    return lax.fori_loop(0, place, one, state)


def local_retention(queries, keys, values, log_decay, block):
    tokens, heads, width = queries.shape
    count = tokens // block

    def to_blocks(array):
        return array.reshape((count, block) + array.shape[1:])

    lower = jnp.arange(block)[:, None] >= jnp.arange(block)[None, :]

    def advance(carry, inputs):
        state, offset = carry
        query_block, key_block, value_block, decay_block = inputs
        within = jnp.cumsum(decay_block, axis=0)
        spread = within[:, None, :] - within[None, :, :]
        factor = jnp.where(
            lower[:, :, None], jnp.exp(jnp.where(lower[:, :, None], spread, 0.0)), 0.0
        )
        scores = jnp.einsum(
            "ihd,jhd->hij", query_block, key_block, preferred_element_type=jnp.float32
        )
        weighted = scores * jnp.transpose(factor, (2, 0, 1))
        values_wide = value_block.astype(jnp.float32)
        intra = jnp.einsum("hij,jhd->ihd", weighted, values_wide, precision=HIGHEST)
        query_wide = query_block.astype(jnp.float32)
        carried = jnp.exp(within)[:, :, None] * jnp.einsum(
            "ihd,hde->ihe", query_wide, state, precision=HIGHEST
        )
        ending = within[-1]
        key_wide = key_block.astype(jnp.float32) * jnp.exp(ending[None, :] - within)[:, :, None]
        fresh = jnp.exp(ending)[:, None, None] * state + jnp.einsum(
            "jhd,jhe->hde", key_wide, values_wide, precision=HIGHEST
        )
        return ((fresh, offset + ending), (intra + carried, offset[None, :] + within))

    start = (jnp.zeros((heads, width, width), jnp.float32), jnp.zeros((heads,), jnp.float32))
    final, stacked = lax.scan(
        advance,
        start,
        (to_blocks(queries), to_blocks(keys), to_blocks(values), to_blocks(log_decay)),
    )
    return (
        stacked[0].reshape(tokens, heads, width),
        stacked[1].reshape(tokens, heads),
        final[0],
        final[1],
    )


def combine_states(earlier, later):
    return (earlier[0] * later[0], later[0][:, None, None] * earlier[1] + later[1])


def on_device(queries, keys, values, gate, residual, log_decay, out_weight, norm_gain, kv_weight):
    tokens = queries.shape[0]
    heads = log_decay.shape[1]
    width = queries.shape[1] // heads
    shaped = [array.reshape(tokens, heads, width) for array in (queries, keys, values)]
    partial_out, running, state, offset = local_retention(
        shaped[0], shaped[1], shaped[2], log_decay, min(512, tokens)
    )
    identity = (jnp.ones((heads,), jnp.float32), jnp.zeros((heads, width, width), jnp.float32))
    scan_decay, incoming = entering((jnp.exp(offset), state), "seq", combine_states, identity)
    retained = partial_out + jnp.exp(running)[:, :, None] * jnp.einsum(
        "thd,hde->the", shaped[0].astype(jnp.float32), incoming, precision=HIGHEST
    )
    scale = lax.rsqrt(jnp.mean(retained * retained, axis=2, keepdims=True) + 1e-06)
    mixed = (
        jax.nn.silu(gate.astype(jnp.float32)) * (retained * scale).reshape(tokens, heads * width)
    ).astype(jnp.bfloat16)
    all_heads = lax.all_gather(mixed, "head", axis=1, tiled=True)
    out_full, kv_full = (
        lax.all_gather(out_weight, "seq", axis=0, tiled=True),
        lax.all_gather(kv_weight, "seq", axis=0, tiled=True),
    )
    branch = jnp.dot(all_heads, out_full, preferred_element_type=jnp.float32)
    hidden = (residual.astype(jnp.float32) + branch).astype(jnp.bfloat16)
    wide = hidden.astype(jnp.float32)
    squares = lax.psum(jnp.sum(wide * wide, axis=1), "head")
    features = wide.shape[1] * lax.axis_size("head")
    inverse = lax.rsqrt(squares[:, None] / features + 1e-06)
    local_norm = (wide * inverse * norm_gain.astype(jnp.float32)[None, :]).astype(jnp.bfloat16)
    normalized = lax.all_gather(local_norm, "head", axis=1, tiled=True)
    projected = jnp.dot(normalized, kv_full, preferred_element_type=jnp.float32)
    cache_heads = kv_weight.shape[1] // (2 * width)
    arranged = projected.reshape(tokens, cache_heads, 2, width)
    cache_keys = arranged[:, :, 0, :].reshape(tokens, cache_heads * width).astype(jnp.bfloat16)
    cache_values = arranged[:, :, 1, :].reshape(tokens, cache_heads * width).astype(jnp.bfloat16)
    return (cache_keys, cache_values)


def solution(mesh):
    placed = (
        P("seq", "head"),
        P("seq", "head"),
        P("seq", "head"),
        P("seq", "head"),
        P("seq", "head"),
        P("seq", "head"),
        P("seq", "head"),
        P("head"),
        P("seq", "head"),
    )
    return jax.shard_map(
        on_device,
        mesh=mesh,
        in_specs=placed,
        out_specs=(P("seq", "head"), P("seq", "head")),
        check_vma=False,
    )
```

profile of v0, /device:TPU:2, one launch (start us, length us, event | category | flops | bytes accessed | tf_op | source)
XLA Modules:
  0.0 390.9 jit_solution(8764286394529594663)
XLA Ops:
  7.2 0.0 copy-start
  7.2 0.0 all-gather.16.cloned.1.call-start
  7.2 0.7 reshape.72
  8.0 1.2 reduce-window.6
  9.2 0.1 slice.23
  9.2 0.1 copy.57
  9.4 0.1 copy.58
  9.5 0.1 add_bitcast_fusion
  9.6 0.2 slice_reduce_fusion
  9.8 0.1 bitcast_exponential_fusion
  9.8 1.1 copy.73
  10.9 2.0 convolution_add_fusion.1
  13.0 0.0 all-gather.16.cloned.1.call-update
  13.0 0.0 all-gather.10.cloned.1.call-start
  13.1 0.7 all-gather.10.cloned.1.call-update
  13.8 0.0 all-gather.8.cloned.1.call-start
  13.8 44.7 %all-gather.1 = f32[64,1,4]{2,1,0:T(1,128)S(1)} all-gather(f32[1,1,4]{2,1,0:T(1,128)S(1)} %bitcast.97), channel_id=1, replica_groups=mesh['seq'=64,'head'=8] {'seq'}, dimensions={0}, use_global_device_ids=true | all-gather | bytes 1040 | tf_op jit(solution)/shard_map/all_gather | solution.py:11
  58.6 0.0 copy-done
  58.6 0.4 fusion.2
  59.0 0.4 convolution_multiply_fusion
  59.4 63.1 %all-gather.16.cloned.1.call-done = f32[256,128,128]{2,1,0:T(8,128)} async-done(((f32[4,128,128]{2,1,0:T(8,128)}), f32[256,128,128]{2,1,0:T(8,128)}) %all-gather.16.cloned.1.call-update) | async-done | bytes 16777232 | tf_op jit(solution)/shard_map/all_gather | solution.py:11
  122.5 0.0 copy-start.1
  122.5 17.8 %while.3 = (s32[]{:T(128)}, f32[4,128,128]{2,1,0:T(8,128)S(1)}, s32[]{:T(128)}, f32[64,4]{1,0:T(8,128)S(1)}, f32[64,4,128,128]{3,2,1,0:T(8,128)}, /*index=5*/s32[]{:T(128)}, s32[]{:T(128)}, s32[]{:T(128)}) while((s32[]{:T(128)}, f32[4,128,128]{2,1,0:T(8,128)S(1)}, s32[]{:T(128)}, f32[64,4]{1,0:T(8,128)S(1)}, f32[64,4,128,128]{3,2,1,0:T(8,128)}, ...), condition=%wide.region_3.4_spmd, body=%wide.region_2.3_spmd.sunk | while | flops 131077 | bytes 786607 | solution.py:19
  122.6 1.1 bitcast_add_fusion.2
  123.7 1.1 bitcast_add_fusion.2
  124.8 1.1 bitcast_add_fusion.2
  125.9 1.1 bitcast_add_fusion.2
  127.0 1.1 bitcast_add_fusion.2
  128.1 1.1 bitcast_add_fusion.2
  129.2 1.1 bitcast_add_fusion.2
  130.4 1.1 bitcast_add_fusion.2
  131.5 1.1 bitcast_add_fusion.2
  132.6 1.1 bitcast_add_fusion.2
  133.7 1.1 bitcast_add_fusion.2
  134.8 1.1 bitcast_add_fusion.2
  135.9 1.1 bitcast_add_fusion.2
  137.0 1.1 bitcast_add_fusion.2
  138.1 1.1 bitcast_add_fusion.2
  139.2 1.1 bitcast_add_fusion.2
  140.3 0.4 fusion.3
  140.7 0.0 copy-done.1
  140.8 0.0 copy-start.2
  140.8 0.8 multiply_reduce_fusion.1
  141.5 0.0 copy-start.3
  141.5 0.0 copy-start.4
  141.6 0.2 copy.66
  141.8 0.0 copy-done.2
  141.8 0.9 fusion.12
  142.7 0.0 all-gather.8.cloned.1.call-update
  142.7 0.0 all-gather.14.cloned.1.call-start
  142.8 0.5 all-gather.14.cloned.1.call-update
  143.3 0.0 all-gather.12.cloned.1.call-start
  143.3 0.0 copy-done.3
  143.4 64.4 %all-gather.10.cloned.1.call-done = bf16[4096,512]{1,0:T(8,128)(2,1)} async-done(((bf16[64,512]{1,0:T(8,128)(2,1)}), bf16[4096,512]{1,0:T(8,128)(2,1)}) %all-gather.10.cloned.1.call-update) | async-done | bytes 4194320 | tf_op jit(solution)/shard_map/all_gather | solution.py:93
  207.8 43.4 %all-gather.8.cloned.1.call-done = bf16[256,4096]{1,0:T(8,128)(2,1)} async-done(((bf16[256,512]{1,0:T(8,128)(2,1)}), bf16[256,4096]{1,0:T(8,128)(2,1)}) %all-gather.8.cloned.1.call-update) | async-done | bytes 2097168 | tf_op jit(solution)/shard_map/all_gather | solution.py:91
  251.2 4.2 %multiply_reduce_fusion = (f32[256]{0:T(256)S(1)}, f32[256,512]{1,0:T(8,128)S(1)}) fusion(bf16[256,4096]{1,0:T(8,128)(2,1)} %all-gather.8.cloned.1.call-done, bf16[4096,512]{1,0:T(8,128)(2,1)} %all-gather.10.cloned.1.call-done, bf16[256,512]{1,0:T(8,128)(2,1)S(1)} %copy-done.4), kind=kOutput, calls=%fused_computation.22 | convolution fusion | flops 1074528000 | bytes 7078912 | tf_op jit(solution)/shard_map/dot_general | solution.py:96
  255.3 16.2 %psum.7 = f32[256]{0:T(256)S(1)} all-reduce(f32[256]{0:T(256)S(1)} %get-tuple-element.97), channel_id=1, replica_groups=mesh['seq'=64,'head'=8] {'head'}, use_global_device_ids=true, to_apply=%region_6.7 | all-reduce | flops 256 | bytes 2048 | tf_op jit(solution)/shard_map/psum | solution.py:99
  271.6 0.8 multiply_convert_fusion
  272.4 0.0 all-gather.12.cloned.1.call-update
  272.4 63.8 %all-gather.14.cloned.1.call-done = bf16[4096,256]{1,0:T(8,128)(2,1)} async-done(((bf16[64,256]{1,0:T(8,128)(2,1)}), bf16[4096,256]{1,0:T(8,128)(2,1)}) %all-gather.14.cloned.1.call-update) | async-done | bytes 2097168 | tf_op jit(solution)/shard_map/all_gather | solution.py:94
  336.2 43.6 %all-gather.12.cloned.1.call-done = bf16[256,4096]{1,0:T(8,128)(2,1)} async-done(((bf16[256,512]{1,0:T(8,128)(2,1)}), bf16[256,4096]{1,0:T(8,128)(2,1)}) %all-gather.12.cloned.1.call-update) | async-done | bytes 2097168 | tf_op jit(solution)/shard_map/all_gather | solution.py:103
  379.8 3.1 convolution_convert_fusion
  382.9 0.7 copy.71
  383.7 0.7 copy.72
  (28 shorter events, 0.3 us)
Async XLA Ops:
  7.2 51.4 %copy-start = (bf16[256,512]{1,0:T(8,128)(2,1)S(1)}, bf16[256,512]{1,0:T(8,128)(2,1)}, u32[]{:S(2)}) copy-start(bf16[256,512]{1,0:T(8,128)(2,1)} %param.11) | copy-start | bytes 786436
  7.2 115.3 %all-gather.16.cloned.1.call-start = ((), (), s32[]{:S(2)}) async-start(), calls=%async_computation.4 | async-start | bytes 17039360 | tf_op jit(solution)/shard_map/all_gather | solution.py:11
  13.0 194.8 %all-gather.10.cloned.1.call-start = ((), (), s32[]{:S(2)}) async-start(), calls=%async_computation.1 | async-start | bytes 4259840 | tf_op jit(solution)/shard_map/all_gather | solution.py:93
  13.8 237.4 %all-gather.8.cloned.1.call-start = ((), (), s32[]{:S(2)}) async-start(), calls=%async_computation | async-start | bytes 2359296 | tf_op jit(solution)/shard_map/all_gather | solution.py:91
  122.5 18.2 %copy-start.1 = (bf16[256,512]{1,0:T(8,128)(2,1)S(1)}, bf16[256,512]{1,0:T(8,128)(2,1)}, u32[]{:S(2)}) copy-start(bf16[256,512]{1,0:T(8,128)(2,1)} %param.13) | copy-start | bytes 786436
  140.8 1.1 copy-start.2
  141.5 1.8 copy-start.3
  141.5 109.7 %copy-start.4 = (bf16[256,512]{1,0:T(8,128)(2,1)S(1)}, bf16[256,512]{1,0:T(8,128)(2,1)}, u32[]{:S(2)}) copy-start(bf16[256,512]{1,0:T(8,128)(2,1)} %param.15) | copy-start | bytes 786436
  142.7 193.4 %all-gather.14.cloned.1.call-start = ((), (), s32[]{:S(2)}) async-start(), calls=%async_computation.3 | async-start | bytes 2129920 | tf_op jit(solution)/shard_map/all_gather | solution.py:94
  143.3 236.5 %all-gather.12.cloned.1.call-start = ((), (), s32[]{:S(2)}) async-start(), calls=%async_computation.2 | async-start | bytes 2359296 | tf_op jit(solution)/shard_map/all_gather | solution.py:103
Sparse Core Ops, SparseCore 0:
  13.1 109.3 all-gather.15
  125.8 81.8 all-gather.9
  209.9 41.2 all-gather.7
  254.4 81.7 all-gather.13
  338.1 41.6 all-gather.11
where the time goes:
time: 393 us; the launch traced here: 391 us
  waiting for transfers between devices  280 us (71%)
  blocking collectives  60.9 us (15%)
  other arithmetic  20.2 us (5%)
  between operations  14 us (4%)
  matrix products  11.3 us (3%)
  local copies, waits for them, and re-layouts  4.19 us (1%)
    all_gather x1, waiting for transfers between devices, on_device(): lax.all_gather(out_weight, 'seq', axis=0, tiled=True)  64.4 us
    all_gather x1, waiting for transfers between devices, on_device(): lax.all_gather(kv_weight, 'seq', axis=0, tiled=True)  63.8 us
    all_gather x1, waiting for transfers between devices, entering(): gathered = jax.tree.map(lambda a: lax.all_gather(a, axis), part)  63.1 us
    all_gather x1, blocking collectives, entering(): gathered = jax.tree.map(lambda a: lax.all_gather(a, axis), part)  44.7 us
    all_gather x1, waiting for transfers between devices, on_device(): normalized = lax.all_gather(local_norm, 'head', axis=1, tiled=True)  43.6 us
    all_gather x1, waiting for transfers between devices, on_device(): all_heads = lax.all_gather(mixed, 'head', axis=1, tiled=True)  43.4 us
    add x16, other arithmetic, combine_states(): later[0][:, None, None] * earlier[1] + later[1]  17 us
    psum x1, blocking collectives, on_device(): squares = lax.psum(jnp.sum(wide * wide, axis=1), 'head')  16.2 us
  transfers between devices with their start and end apart: 5, of which 5 were waited for; matrix products, arithmetic and copies ran while one was open for 6% of the time, Pallas kernels for 0%

commit v1 on v0

--- a/solution.py
+++ b/solution.py
@@ -4,6 +4,34 @@
 from jax.sharding import PartitionSpec as P
 
 HIGHEST = lax.Precision.HIGHEST
+
+
+def _state_panel(load, peer_axis):
+    local_out = lax.axis_size(peer_axis)
+    e_next = lax.axis_index(peer_axis)
+    local_next, newest, k_now = (local_out, e_next, load.shape[1])
+    near = lax.dynamic_update_slice_in_dim(
+        jnp.zeros([p * local_next if b == 1 else p for b, p in enumerate(load.shape)], load.dtype),
+        load,
+        newest * k_now,
+        axis=1,
+    )
+    aux = z2 = load
+    ix = 1
+    while ix < local_next // 2 + 1:
+        aux = lax.ppermute(aux, peer_axis, [(b, (b + 1) % local_next) for b in range(local_next)])
+        near = lax.dynamic_update_slice_in_dim(
+            near, aux, (newest - ix) % local_next * k_now, axis=1
+        )
+        if 2 * ix < local_next:
+            z2 = lax.ppermute(
+                z2, peer_axis, perm=[(b, (b - 1) % local_next) for b in range(local_next)]
+            )
+            near = lax.dynamic_update_slice_in_dim(
+                near, z2, (newest + ix) % local_next * k_now, axis=1
+            )
+        ix += 1
+    return near
 
 
 def entering(part, axis, combine, identity):
@@ -100,7 +128,7 @@
     features = wide.shape[1] * lax.axis_size("head")
     inverse = lax.rsqrt(squares[:, None] / features + 1e-06)
     local_norm = (wide * inverse * norm_gain.astype(jnp.float32)[None, :]).astype(jnp.bfloat16)
-    normalized = lax.all_gather(local_norm, "head", axis=1, tiled=True)
+    normalized = _state_panel(local_norm, "head")
     projected = jnp.dot(normalized, kv_full, preferred_element_type=jnp.float32)
     cache_heads = kv_weight.shape[1] // (2 * width)
     arranged = projected.reshape(tokens, cache_heads, 2, width)

time: 393 us -> 351 us (0.89)
  the two profiles are of different devices: /device:TPU:2 before, /device:TPU:1 now
where the time goes in v1:
time: 351 us; the launch traced here: 349 us
  waiting for transfers between devices  235 us (67%)
  blocking collectives  58.4 us (17%)
  starting transfers between devices  22.2 us (6%)
  between operations  14.2 us (4%)
  matrix products  10.7 us (3%)
  local copies, waits for them, and re-layouts  4.46 us (1%)
  other arithmetic  3.56 us (1%)
    all_gather x1, waiting for transfers between devices, on_device(): lax.all_gather(out_weight, 'seq', axis=0, tiled=True)  80.9 us
    all_gather x1, waiting for transfers between devices, entering(): gathered = jax.tree.map(lambda a: lax.all_gather(a, axis), part)  64 us
    all_gather x1, blocking collectives, entering(): gathered = jax.tree.map(lambda a: lax.all_gather(a, axis), part)  46.4 us
    all_gather x1, waiting for transfers between devices, on_device(): all_heads = lax.all_gather(mixed, 'head', axis=1, tiled=True)  38.3 us
    all_gather x1, waiting for transfers between devices, on_device(): lax.all_gather(kv_weight, 'seq', axis=0, tiled=True)  35.6 us
    ppermute x4, waiting for transfers between devices, _state_panel(): lax.ppermute(aux, peer_axis, [(b, (b + 1) % local_next) for b in range(lo...  15.3 us
    ppermute x3, starting transfers between devices, _state_panel(): lax.ppermute(z2, peer_axis, perm=[(b, (b - 1) % local_next) for b in rang...  14.3 us
    psum x1, blocking collectives, on_device(): squares = lax.psum(jnp.sum(wide * wide, axis=1), 'head')  12 us
  transfers between devices with their start and end apart: 11, of which 8 were waited for; matrix products, arithmetic and copies ran while one was open for 3% of the time, Pallas kernels for 0%

profile of v1, /device:TPU:1, one launch (start us, length us, event | category | flops | bytes accessed | tf_op | source)
XLA Modules:
  0.0 348.8 jit_solution(12634482392994203355)
XLA Ops:
  7.2 0.0 copy-start
  7.2 0.0 all-gather.13.cloned.1.call-start
  7.2 0.7 reshape.72
  8.0 1.2 reduce-window.6
  9.2 0.1 slice.23
  9.2 0.1 copy.57
  9.4 0.1 copy.58
  9.5 0.1 add_bitcast_fusion
  9.6 0.2 slice_reduce_fusion
  9.8 0.1 bitcast_exponential_fusion
  9.8 1.1 copy.73
  10.9 2.0 convolution_add_fusion.1
  13.0 0.0 all-gather.13.cloned.1.call-update
  13.0 0.0 all-gather.9.cloned.1.call-start
  13.1 0.7 all-gather.9.cloned.1.call-update
  13.8 0.0 all-gather.7.cloned.1.call-start
  13.8 46.4 %all-gather.1 = f32[64,1,4]{2,1,0:T(1,128)S(1)} all-gather(f32[1,1,4]{2,1,0:T(1,128)S(1)} %bitcast.97), channel_id=1, replica_groups=mesh['seq'=64,'head'=8] {'seq'}, dimensions={0}, use_global_device_ids=true | all-gather | bytes 1040 | tf_op jit(solution)/shard_map/all_gather | solution.py:39
  60.2 0.0 copy-done
  60.2 0.4 fusion.2
  60.6 0.4 convolution_multiply_fusion
  61.0 64.0 %all-gather.13.cloned.1.call-done = f32[256,128,128]{2,1,0:T(8,128)} async-done(((f32[4,128,128]{2,1,0:T(8,128)}), f32[256,128,128]{2,1,0:T(8,128)}) %all-gather.13.cloned.1.call-update) | async-done | bytes 16777232 | tf_op jit(solution)/shard_map/all_gather | solution.py:39
  125.0 0.0 copy-start.1
  125.0 1.1 while.3
  125.1 1.1 bitcast_add_fusion.2
  126.2 0.4 fusion.3
  126.6 0.0 copy-done.1
  126.6 0.0 copy-start.2
  126.7 0.8 multiply_reduce_fusion.1
  127.4 0.0 copy-start.3
  127.4 0.0 copy-start.4
  127.5 0.2 copy.66
  127.7 0.0 copy-done.2
  127.7 0.9 fusion.12
  128.6 0.0 all-gather.7.cloned.1.call-update
  128.6 0.0 all-gather.11.cloned.1.call-start
  128.7 0.5 all-gather.11.cloned.1.call-update
  129.2 0.0 copy-done.3
  129.2 80.9 %all-gather.9.cloned.1.call-done = bf16[4096,512]{1,0:T(8,128)(2,1)} async-done(((bf16[64,512]{1,0:T(8,128)(2,1)}), bf16[4096,512]{1,0:T(8,128)(2,1)}) %all-gather.9.cloned.1.call-update) | async-done | bytes 4194320 | tf_op jit(solution)/shard_map/all_gather | solution.py:121
  210.1 38.3 %all-gather.7.cloned.1.call-done = bf16[256,4096]{1,0:T(8,128)(2,1)} async-done(((bf16[256,512]{1,0:T(8,128)(2,1)}), bf16[256,4096]{1,0:T(8,128)(2,1)}) %all-gather.7.cloned.1.call-update) | async-done | bytes 2097168 | tf_op jit(solution)/shard_map/all_gather | solution.py:119
  248.4 0.0 copy-done.4
  248.4 4.2 %multiply_reduce_fusion = (f32[256]{0:T(256)S(1)}, f32[256,512]{1,0:T(8,128)S(1)}) fusion(bf16[256,4096]{1,0:T(8,128)(2,1)} %all-gather.7.cloned.1.call-done, bf16[4096,512]{1,0:T(8,128)(2,1)} %all-gather.9.cloned.1.call-done, bf16[256,512]{1,0:T(8,128)(2,1)S(1)} %copy-done.4), kind=kOutput, calls=%fused_computation.22 | convolution fusion | flops 1074528000 | bytes 7078912 | tf_op jit(solution)/shard_map/dot_general | solution.py:124
  252.5 12.0 %psum.7 = f32[256]{0:T(256)S(1)} all-reduce(f32[256]{0:T(256)S(1)} %get-tuple-element.99), channel_id=1, replica_groups=mesh['seq'=64,'head'=8] {'head'}, use_global_device_ids=true, to_apply=%region_6.7 | all-reduce | flops 256 | bytes 2048 | tf_op jit(solution)/shard_map/psum | solution.py:127
  264.5 0.2 broadcast_in_dim.56
  264.8 0.1 constant_dynamic-update-slice_fusion.7
  264.9 2.0 collective-permute-start
  266.9 4.5 %collective-permute-start.1 = (bf16[256,512]{1,0:T(8,128)(2,1)S(1)}, bf16[256,512]{1,0:T(8,128)(2,1)S(1)}, u32[]{:S(2)}, u32[]{:S(2)}) collective-permute-start(bf16[256,512]{1,0:T(8,128)(2,1)S(1)} %get-tuple-element.90), channel_id=1, source_target_pairs={{0,7},{1,0},{2,1},{3,2},{4,3},{5,4},{6,5},{7,6},{8,15},{9,8},{10,9... | collective-permute-start | bytes 786440 | tf_op jit(solution)/shard_map/ppermute | solution.py:27
  271.4 1.9 collective-permute-done
  273.3 1.9 collective-permute-start.2
  275.2 0.0 collective-permute-done.1
  275.2 4.9 %collective-permute-start.3 = (bf16[256,512]{1,0:T(8,128)(2,1)S(1)}, bf16[256,512]{1,0:T(8,128)(2,1)S(1)}, u32[]{:S(2)}, u32[]{:S(2)}) collective-permute-start(bf16[256,512]{1,0:T(8,128)(2,1)S(1)} %collective-permute-done.1), channel_id=1, source_target_pairs={{0,7},{1,0},{2,1},{3,2},{4,3},{5,4},{6,5},{7,6},{8,15},{9,8},{10,9... | collective-permute-start | bytes 786440 | tf_op jit(solution)/shard_map/ppermute | solution.py:27
  280.3 3.7 %collective-permute-done.2 = bf16[256,512]{1,0:T(8,128)(2,1)S(1)} collective-permute-done((bf16[256,512]{1,0:T(8,128)(2,1)S(1)}, bf16[256,512]{1,0:T(8,128)(2,1)S(1)}, u32[]{:S(2)}, u32[]{:S(2)}) %collective-permute-start.2) | collective-permute-done | bytes 262176 | tf_op jit(solution)/shard_map/ppermute | solution.py:22
  284.0 1.9 collective-permute-start.4
  286.0 0.0 collective-permute-done.3
  286.0 4.9 %collective-permute-start.5 = (bf16[256,512]{1,0:T(8,128)(2,1)S(1)}, bf16[256,512]{1,0:T(8,128)(2,1)S(1)}, u32[]{:S(2)}, u32[]{:S(2)}) collective-permute-start(bf16[256,512]{1,0:T(8,128)(2,1)S(1)} %collective-permute-done.3), channel_id=1, source_target_pairs={{0,7},{1,0},{2,1},{3,2},{4,3},{5,4},{6,5},{7,6},{8,15},{9,8},{10,9... | collective-permute-start | bytes 786440 | tf_op jit(solution)/shard_map/ppermute | solution.py:27
  291.0 2.8 collective-permute-done.4
  293.8 1.9 collective-permute-start.6
  295.8 0.0 collective-permute-done.5
  295.8 6.8 %collective-permute-done.6 = bf16[256,512]{1,0:T(8,128)(2,1)S(1)} collective-permute-done((bf16[256,512]{1,0:T(8,128)(2,1)S(1)}, bf16[256,512]{1,0:T(8,128)(2,1)S(1)}, u32[]{:S(2)}, u32[]{:S(2)}) %collective-permute-start.6) | collective-permute-done | bytes 262176 | tf_op jit(solution)/shard_map/ppermute | solution.py:22
  302.7 35.6 %all-gather.11.cloned.1.call-done = bf16[4096,256]{1,0:T(8,128)(2,1)} async-done(((bf16[64,256]{1,0:T(8,128)(2,1)}), bf16[4096,256]{1,0:T(8,128)(2,1)}) %all-gather.11.cloned.1.call-update) | async-done | bytes 2097168 | tf_op jit(solution)/shard_map/all_gather | solution.py:122
  338.3 2.5 convolution_convert_fusion
  340.8 0.7 copy.71
  341.6 0.7 copy.72
  (19 shorter events, 0.4 us)
Async XLA Ops:
  7.2 53.0 %copy-start = (bf16[256,512]{1,0:T(8,128)(2,1)S(1)}, bf16[256,512]{1,0:T(8,128)(2,1)}, u32[]{:S(2)}) copy-start(bf16[256,512]{1,0:T(8,128)(2,1)} %param.11) | copy-start | bytes 786436
  7.2 117.8 %all-gather.13.cloned.1.call-start = ((), (), s32[]{:S(2)}) async-start(), calls=%async_computation.3 | async-start | bytes 17039360 | tf_op jit(solution)/shard_map/all_gather | solution.py:39
  13.0 197.1 %all-gather.9.cloned.1.call-start = ((), (), s32[]{:S(2)}) async-start(), calls=%async_computation.1 | async-start | bytes 4259840 | tf_op jit(solution)/shard_map/all_gather | solution.py:121
  13.8 234.6 %all-gather.7.cloned.1.call-start = ((), (), s32[]{:S(2)}) async-start(), calls=%async_computation | async-start | bytes 2359296 | tf_op jit(solution)/shard_map/all_gather | solution.py:119
  125.0 1.6 copy-start.1
  126.6 1.1 copy-start.2
  127.4 1.8 copy-start.3
  127.4 120.9 %copy-start.4 = (bf16[256,512]{1,0:T(8,128)(2,1)S(1)}, bf16[256,512]{1,0:T(8,128)(2,1)}, u32[]{:S(2)}) copy-start(bf16[256,512]{1,0:T(8,128)(2,1)} %param.15) | copy-start | bytes 786436
  128.6 209.7 %all-gather.11.cloned.1.call-start = ((), (), s32[]{:S(2)}) async-start(), calls=%async_computation.2 | async-start | bytes 2129920 | tf_op jit(solution)/shard_map/all_gather | solution.py:122
  264.9 8.4 %collective-permute-start = (bf16[256,512]{1,0:T(8,128)(2,1)S(1)}, bf16[256,512]{1,0:T(8,128)(2,1)S(1)}, u32[]{:S(2)}, u32[]{:S(2)}) collective-permute-start(bf16[256,512]{1,0:T(8,128)(2,1)S(1)} %get-tuple-element.90), channel_id=1, source_target_pairs={{0,1},{1,2},{2,3},{3,4},{4,5},{5,6},{6,7},{7,0},{8,9},{9,10},{10,1... | collective-permute-start | bytes 786440 | tf_op jit(solution)/shard_map/ppermute | solution.py:22
  266.9 8.3 %collective-permute-start.1 = (bf16[256,512]{1,0:T(8,128)(2,1)S(1)}, bf16[256,512]{1,0:T(8,128)(2,1)S(1)}, u32[]{:S(2)}, u32[]{:S(2)}) collective-permute-start(bf16[256,512]{1,0:T(8,128)(2,1)S(1)} %get-tuple-element.90), channel_id=1, source_target_pairs={{0,7},{1,0},{2,1},{3,2},{4,3},{5,4},{6,5},{7,6},{8,15},{9,8},{10,9... | collective-permute-start | bytes 786440 | tf_op jit(solution)/shard_map/ppermute | solution.py:27
  273.3 10.7 %collective-permute-start.2 = (bf16[256,512]{1,0:T(8,128)(2,1)S(1)}, bf16[256,512]{1,0:T(8,128)(2,1)S(1)}, u32[]{:S(2)}, u32[]{:S(2)}) collective-permute-start(bf16[256,512]{1,0:T(8,128)(2,1)S(1)} %collective-permute-done), channel_id=1, source_target_pairs={{0,1},{1,2},{2,3},{3,4},{4,5},{5,6},{6,7},{7,0},{8,9},{9,10},{10,1... | collective-permute-start | bytes 786440 | tf_op jit(solution)/shard_map/ppermute | solution.py:22
  275.2 10.8 %collective-permute-start.3 = (bf16[256,512]{1,0:T(8,128)(2,1)S(1)}, bf16[256,512]{1,0:T(8,128)(2,1)S(1)}, u32[]{:S(2)}, u32[]{:S(2)}) collective-permute-start(bf16[256,512]{1,0:T(8,128)(2,1)S(1)} %collective-permute-done.1), channel_id=1, source_target_pairs={{0,7},{1,0},{2,1},{3,2},{4,3},{5,4},{6,5},{7,6},{8,15},{9,8},{10,9... | collective-permute-start | bytes 786440 | tf_op jit(solution)/shard_map/ppermute | solution.py:27
  284.0 9.8 %collective-permute-start.4 = (bf16[256,512]{1,0:T(8,128)(2,1)S(1)}, bf16[256,512]{1,0:T(8,128)(2,1)S(1)}, u32[]{:S(2)}, u32[]{:S(2)}) collective-permute-start(bf16[256,512]{1,0:T(8,128)(2,1)S(1)} %collective-permute-done.2), channel_id=1, source_target_pairs={{0,1},{1,2},{2,3},{3,4},{4,5},{5,6},{6,7},{7,0},{8,9},{9,10},{10,1... | collective-permute-start | bytes 786440 | tf_op jit(solution)/shard_map/ppermute | solution.py:22
  286.0 9.8 %collective-permute-start.5 = (bf16[256,512]{1,0:T(8,128)(2,1)S(1)}, bf16[256,512]{1,0:T(8,128)(2,1)S(1)}, u32[]{:S(2)}, u32[]{:S(2)}) collective-permute-start(bf16[256,512]{1,0:T(8,128)(2,1)S(1)} %collective-permute-done.3), channel_id=1, source_target_pairs={{0,7},{1,0},{2,1},{3,2},{4,3},{5,4},{6,5},{7,6},{8,15},{9,8},{10,9... | collective-permute-start | bytes 786440 | tf_op jit(solution)/shard_map/ppermute | solution.py:27
  293.8 8.9 %collective-permute-start.6 = (bf16[256,512]{1,0:T(8,128)(2,1)S(1)}, bf16[256,512]{1,0:T(8,128)(2,1)S(1)}, u32[]{:S(2)}, u32[]{:S(2)}) collective-permute-start(bf16[256,512]{1,0:T(8,128)(2,1)S(1)} %collective-permute-done.4), channel_id=1, source_target_pairs={{0,1},{1,2},{2,3},{3,4},{4,5},{5,6},{6,7},{7,0},{8,9},{9,10},{10,1... | collective-permute-start | bytes 786440 | tf_op jit(solution)/shard_map/ppermute | solution.py:22
Sparse Core Ops, SparseCore 0:
  13.1 111.8 all-gather.12
  128.4 81.6 all-gather.8
  212.2 36.1 all-gather.6
  251.6 86.6 all-gather.10
